TPU v7x, 512 devices: a whole 4x8x8 slice. The times are simulated.
512 devices in a mesh: seq: 64 (over z_hi, y, core), head: 8 (over x, z_lo).
Axes of the slice: x: 4, y: 8, z: 8 (z_hi: 4, z_lo: 2; z = z_hi * 2 + z_lo), core: 2. Of those that a mesh axis runs over, the one named last changes fastest.
Arguments:
- target: bfloat16 [16384, 2048], P('seq', 'head'), may hold values from -1000 to 1000, as said below
- source: bfloat16 [16384, 2048], P('seq', 'head'), may hold values from -6 to 6
- w_query: bfloat16 [2048, 2048], P('seq', 'head'), may hold values from -0.125 to 0.125
- w_key: bfloat16 [2048, 2048], P('seq', 'head'), may hold values from -0.125 to 0.125
- w_value: bfloat16 [2048, 2048], P('seq', 'head'), may hold values from -0.125 to 0.125
- w_out: bfloat16 [2048, 2048], P('seq', 'head'), may hold values from -0.125 to 0.125
- band_start: int32 [256], P('seq'), may hold values from 0 to 255, as said below
- band_end: int32 [256], P('seq'), may hold values from 1 to 256, as said below
- cotangent: bfloat16 [16384, 2048], P('seq', 'head'), may hold values from -6 to 6
Outputs:
- attended: bfloat16 [16384, 2048], P('seq', 'head')
- grad_target: bfloat16 [16384, 2048], P('seq', 'head')
- grad_source: bfloat16 [16384, 2048], P('seq', 'head')
Inputs may be any that keep to these rules, and one draw needn't show every extreme that they name: `target`: activations of order one, at most some rows much larger. band_start and band_end never fall from block to block; band_start[b] >= b - 1, band_start[b] < band_end[b] <= band_start[b] + 3, band_end[b] <= b + 3; some target block has a band of exactly 3 source blocks. `band_end`: see band_start.
All inputs are finite; a program needn't handle non-finite values.
Results may differ from a plain program's by a relative error of at most 0.02.
Values may be sent and summed in bfloat16 or wider, within the bound.
No kernel may reach another device: no remote copies, remote signals or barrier semaphores. Data moves between devices by JAX's collectives and lax.ppermute only.
A program may use at most 64 MiB of HBM per device.

v0:
```python
import jax
import jax.numpy as jnp
from jax import lax
from jax.sharding import PartitionSpec as P

HEAD_DIM = 128
BLOCK = 64
MAXW = 3


def passed_along(shard, axis, by):
    count = lax.axis_size(axis)
    pairs = [(i, i + by) for i in range(count) if 0 <= i + by < count]
    return lax.ppermute(shard, axis, pairs)


def fold_rows(weight, piece):
    return jnp.dot(piece, weight, preferred_element_type=jnp.float32)


def times_transpose(left, right):
    return lax.dot_general(
        left, right, (((1,), (1,)), ((), ())), preferred_element_type=jnp.float32
    )


def per_device(target, source, w_query, w_key, w_value, w_out, band_start, band_end, cotangent):
    fone = jnp.float32
    half = jnp.bfloat16
    rows = target.shape[0]
    width = w_query.shape[1]
    heads = width // HEAD_DIM
    blocks = rows // BLOCK
    right_rows = (MAXW - 1) * BLOCK
    scale = HEAD_DIM ** (-0.5)
    wq, wk, wv, wo = (
        lax.all_gather(w_query, "seq", axis=0, tiled=True),
        lax.all_gather(w_key, "seq", axis=0, tiled=True),
        lax.all_gather(w_value, "seq", axis=0, tiled=True),
        lax.all_gather(w_out, "seq", axis=0, tiled=True),
    )
    query = fold_rows(wq, lax.all_gather(target, "head", axis=1, tiled=True)).astype(half)
    piece = lax.all_gather(source, "head", axis=1, tiled=True)
    key_sum = fold_rows(wk, piece)
    value_sum = fold_rows(wv, piece)
    packed = jnp.concatenate([key_sum.astype(half), value_sum.astype(half)], 1)
    from_prev = passed_along(packed[rows - BLOCK :], "seq", 1)
    from_next = passed_along(packed[:right_rows], "seq", -1)
    window = jnp.concatenate([from_prev, packed, from_next], 0)
    span_all = window.shape[0]
    anchor = lax.axis_index("seq") * blocks - 1
    low = band_start - anchor
    high = band_end - anchor
    count = 1
    q_blocks = query.reshape(1, rows, heads, HEAD_DIM)
    kv_blocks = window.reshape(1, span_all, 2 * heads, HEAD_DIM)
    key_block = (jnp.arange(span_all, dtype=jnp.int32) // BLOCK)[None, :]
    low_rows = jnp.repeat(low, BLOCK)[None, :]
    high_rows = jnp.repeat(high, BLOCK)[None, :]
    k_blocks = kv_blocks[:, :, :heads]
    v_blocks = kv_blocks[:, :, heads:]
    visible = (key_block[:, None, :] >= low_rows[:, :, None]) & (
        key_block[:, None, :] < high_rows[:, :, None]
    )
    scores = jnp.einsum("nqhe,nkhe->nhqk", q_blocks, k_blocks, preferred_element_type=fone) * scale
    scores = jnp.where(visible[:, None], scores, -jnp.inf)
    top = jnp.max(scores, axis=-1, keepdims=True)
    expo = jnp.exp(scores - top)
    prob = expo / jnp.sum(expo, axis=-1, keepdims=True)
    prob_b = prob.astype(half)
    context = jnp.einsum("nhqk,nkhe->nqhe", prob_b, v_blocks, preferred_element_type=fone).astype(
        half
    )
    context_flat = context.reshape(rows, width)
    attended = (
        lax.psum_scatter(
            times_transpose(context_flat, wo).astype(jnp.bfloat16),
            "head",
            scatter_dimension=1,
            tiled=True,
        )
        .astype(jnp.float32)
        .astype(half)
    )
    d_context = fold_rows(wo, lax.all_gather(cotangent, "head", axis=1, tiled=True)).astype(half)
    dc_blocks = d_context.reshape(context.shape)
    delta = jnp.sum(dc_blocks.astype(fone) * context.astype(fone), axis=-1)
    delta = jnp.transpose(delta, (0, 2, 1))[..., None]
    d_prob = jnp.einsum("nqhe,nkhe->nhqk", dc_blocks, v_blocks, preferred_element_type=fone)
    d_score = (prob * (d_prob - delta) * scale).astype(half)
    d_query = jnp.einsum("nhqk,nkhe->nqhe", d_score, k_blocks, preferred_element_type=fone).astype(
        half
    )
    dk_blocks = jnp.einsum("nhqk,nqhe->nkhe", d_score, q_blocks, preferred_element_type=fone)
    dv_blocks = jnp.einsum("nhqk,nqhe->nkhe", prob_b, dc_blocks, preferred_element_type=fone)
    dkv_blocks = jnp.concatenate(
        [dk_blocks.reshape(count, span_all, width), dv_blocks.reshape(count, span_all, width)], 2
    )
    dkv_window = dkv_blocks.reshape(span_all, 2 * width)
    back_next = passed_along(dkv_window[:BLOCK], "seq", -1)
    back_prev = passed_along(dkv_window[BLOCK + rows :], "seq", 1)
    owned = dkv_window[BLOCK : BLOCK + rows]
    owned = owned.at[rows - BLOCK :].add(back_next)
    owned = owned.at[:right_rows].add(back_prev)
    d_key = owned[:, :width].astype(half)
    d_value = owned[:, width:].astype(half)
    d_query_flat = d_query.reshape(rows, width)
    grad_target = (
        lax.psum_scatter(
            times_transpose(d_query_flat, wq).astype(jnp.bfloat16),
            "head",
            scatter_dimension=1,
            tiled=True,
        )
        .astype(jnp.float32)
        .astype(half)
    )
    source_term = times_transpose(d_key, wk) + times_transpose(d_value, wv)
    grad_source = (
        lax.psum_scatter(source_term.astype(jnp.bfloat16), "head", scatter_dimension=1, tiled=True)
        .astype(jnp.float32)
        .astype(half)
    )
    return (attended, grad_target, grad_source)


def solution(mesh):
    in_specs = (
        P("seq", "head"),
        P("seq", "head"),
        P("seq", "head"),
        P("seq", "head"),
        P("seq", "head"),
        P("seq", "head"),
        P("seq"),
        P("seq"),
        P("seq", "head"),
    )
    out_specs = (P("seq", "head"), P("seq", "head"), P("seq", "head"))
    return jax.shard_map(
        per_device, mesh=mesh, in_specs=in_specs, out_specs=out_specs, check_vma=False
    )
```

profile of v0, /device:TPU:8, one launch (start us, length us, event | category | flops | bytes accessed | tf_op | source)
XLA Modules:
  0.0 650.5 jit_solution(3358592871795059263)
XLA Ops:
  11.2 0.7 all-gather.18.cloned.1.call-update
  13.1 46.8 %all-gather.8.cloned.1.call-done = bf16[256,2048]{1,0:T(8,128)(2,1)} async-done(((bf16[256,256]{1,0:T(8,128)(2,1)}), bf16[256,2048]{1,0:T(8,128)(2,1)}) %all-gather.8.cloned.1.call-update) | async-done | bytes 1048592 | tf_op jit(solution)/shard_map/all_gather | solution.py:43
  59.9 86.9 %all-gather.12.cloned.1.call-done = bf16[2048,256]{1,0:T(8,128)(2,1)} async-done(((bf16[32,256]{1,0:T(8,128)(2,1)}), bf16[2048,256]{1,0:T(8,128)(2,1)}) %all-gather.12.cloned.1.call-update) | async-done | bytes 1048592 | tf_op jit(solution)/shard_map/all_gather | solution.py:39
  146.8 2.1 convolution_convert_fusion.6
  148.9 81.7 %all-gather.10.cloned.1.call-done = bf16[2048,256]{1,0:T(8,128)(2,1)} async-done(((bf16[32,256]{1,0:T(8,128)(2,1)}), bf16[2048,256]{1,0:T(8,128)(2,1)}) %all-gather.10.cloned.1.call-update) | async-done | bytes 1048592 | tf_op jit(solution)/shard_map/all_gather | solution.py:38
  230.6 1.7 convolution_convert_fusion.7
  232.4 2.1 collective-permute-start
  234.6 3.4 collective-permute-start.1
  238.0 37.7 %all-gather.14.cloned.1.call-done = bf16[256,2048]{1,0:T(8,128)(2,1)} async-done(((bf16[256,256]{1,0:T(8,128)(2,1)}), bf16[256,2048]{1,0:T(8,128)(2,1)}) %all-gather.14.cloned.1.call-update) | async-done | bytes 1048592 | tf_op jit(solution)/shard_map/all_gather | solution.py:42
  275.7 86.8 %all-gather.16.cloned.1.call-done = bf16[2048,256]{1,0:T(8,128)(2,1)} async-done(((bf16[32,256]{1,0:T(8,128)(2,1)}), bf16[2048,256]{1,0:T(8,128)(2,1)}) %all-gather.16.cloned.1.call-update) | async-done | bytes 1048592 | tf_op jit(solution)/shard_map/all_gather | solution.py:37
  362.5 2.1 convolution_convert_fusion.5
  364.6 43.1 %all-gather.20.cloned.1.call-done = bf16[256,2048]{1,0:T(8,128)(2,1)} async-done(((bf16[256,256]{1,0:T(8,128)(2,1)}), bf16[256,2048]{1,0:T(8,128)(2,1)}) %all-gather.20.cloned.1.call-update) | async-done | bytes 1048592 | tf_op jit(solution)/shard_map/all_gather | solution.py:85
  407.7 86.9 %all-gather.18.cloned.1.call-done = bf16[2048,256]{1,0:T(8,128)(2,1)} async-done(((bf16[32,256]{1,0:T(8,128)(2,1)}), bf16[2048,256]{1,0:T(8,128)(2,1)}) %all-gather.18.cloned.1.call-update) | async-done | bytes 1048592 | tf_op jit(solution)/shard_map/all_gather | solution.py:40
  494.6 2.1 convolution_convert_fusion.4
  497.5 0.7 fusion.10
  498.7 1.5 convolution_convert_fusion.1
  501.5 1.5 convolution_convert_fusion
  505.0 3.1 collective-permute-start.2
  508.4 2.1 collective-permute-start.3
  511.0 5.2 collective-permute-done.3
  517.5 1.4 fusion.1
  519.0 26.4 %reduce-scatter.4.cloned.1.call-done = bf16[256,256]{1,0:T(8,128)(2,1)} async-done(((bf16[256,2048]{1,0:T(8,128)(2,1)}), bf16[256,256]{1,0:T(8,128)(2,1)}) %reduce-scatter.4.cloned.1.call-update) | async-done | bytes 131088 | tf_op jit(solution)/shard_map/reduce_scatter | solution.py:76
  545.4 49.6 %reduce-scatter.6.cloned.1.call-done = bf16[256,256]{1,0:T(8,128)(2,1)} async-done(((bf16[256,2048]{1,0:T(8,128)(2,1)}), bf16[256,256]{1,0:T(8,128)(2,1)}) %reduce-scatter.6.cloned.1.call-update) | async-done | bytes 131088 | tf_op jit(solution)/shard_map/reduce_scatter | solution.py:109
  595.1 48.6 %reduce-scatter.8.cloned.1.call-done = bf16[256,256]{1,0:T(8,128)(2,1)} async-done(((bf16[256,2048]{1,0:T(8,128)(2,1)}), bf16[256,256]{1,0:T(8,128)(2,1)}) %reduce-scatter.8.cloned.1.call-update) | async-done | bytes 131088 | tf_op jit(solution)/shard_map/reduce_scatter | solution.py:120
  (59 shorter events, 11.8 us)
Async XLA Ops:
  7.2 52.8 %all-gather.8.cloned.1.call-start = ((), (), s32[]{:S(2)}) async-start(), calls=%async_computation.3 | async-start | bytes 1179648 | tf_op jit(solution)/shard_map/all_gather | solution.py:43
  7.9 138.9 %all-gather.12.cloned.1.call-start = ((), (), s32[]{:S(2)}) async-start(), calls=%async_computation.5 | async-start | bytes 1064960 | tf_op jit(solution)/shard_map/all_gather | solution.py:39
  8.6 221.9 %all-gather.10.cloned.1.call-start = ((), (), s32[]{:S(2)}) async-start(), calls=%async_computation.4 | async-start | bytes 1064960 | tf_op jit(solution)/shard_map/all_gather | solution.py:38
  9.4 266.4 %all-gather.14.cloned.1.call-start = ((), (), s32[]{:S(2)}) async-start(), calls=%async_computation.6 | async-start | bytes 1179648 | tf_op jit(solution)/shard_map/all_gather | solution.py:42
  10.0 352.6 %all-gather.16.cloned.1.call-start = ((), (), s32[]{:S(2)}) async-start(), calls=%async_computation.7 | async-start | bytes 1064960 | tf_op jit(solution)/shard_map/all_gather | solution.py:37
  10.5 397.1 %all-gather.20.cloned.1.call-start = ((), (), s32[]{:S(2)}) async-start(), calls=%async_computation.10 | async-start | bytes 1179648 | tf_op jit(solution)/shard_map/all_gather | solution.py:85
  11.1 483.5 %all-gather.18.cloned.1.call-start = ((), (), s32[]{:S(2)}) async-start(), calls=%async_computation.8 | async-start | bytes 1064960 | tf_op jit(solution)/shard_map/all_gather | solution.py:40
  11.9 533.6 %reduce-scatter.4.cloned.1.call-start = ((), (), s32[]{:S(2)}) async-start(), calls=%async_computation.9 | async-start | bytes 1179648 | tf_op jit(solution)/shard_map/reduce_scatter | solution.py:76
  59.9 170.7 %copy-start.2 = (bf16[256,2048]{1,0:T(8,128)(2,1)S(1)}, bf16[256,2048]{1,0:T(8,128)(2,1)}, u32[]{:S(2)}) copy-start(bf16[256,2048]{1,0:T(8,128)(2,1)} %all-gather.8.cloned.1.call-done) | copy-start | bytes 3145732
  232.4 264.3 %collective-permute-start = (bf16[64,512]{0,1:T(8,128)(2,1)S(1)}, bf16[64,512]{0,1:T(8,128)(2,1)S(1)}, u32[]{:S(2)}, u32[]{:S(2)}) collective-permute-start(bf16[64,512]{0,1:T(8,128)(2,1)S(1)} %fusion.13), channel_id=1, source_target_pairs={{0,8},{8,16},{16,24},{24,32},{32,40},{40,48},{48,56},{56,64},{64,7... | collective-permute-start | bytes 196616 | tf_op jit(solution)/shard_map/ppermute | solution.py:14
  234.6 262.1 %collective-permute-start.1 = (bf16[128,512]{0,1:T(8,128)(2,1)S(1)}, bf16[128,512]{0,1:T(8,128)(2,1)S(1)}, u32[]{:S(2)}, u32[]{:S(2)}) collective-permute-start(bf16[128,512]{0,1:T(8,128)(2,1)S(1)} %pad_maximum_fusion.2), channel_id=1, source_target_pairs={{8,0},{16,8},{24,16},{32,24},{40,32},{48,40},{56,48},{64,56},{72,6... | collective-permute-start | bytes 393224 | tf_op jit(solution)/shard_map/ppermute | solution.py:14
  497.5 1.2 copy-start.3
  500.2 94.9 %reduce-scatter.6.cloned.1.call-start = ((), (), s32[]{:S(2)}) async-start(), calls=%async_computation.11 | async-start | bytes 1179648 | tf_op jit(solution)/shard_map/reduce_scatter | solution.py:109
  500.3 1.2 copy-start.1
  503.0 140.7 %reduce-scatter.8.cloned.1.call-start = ((), (), s32[]{:S(2)}) async-start(), calls=%async_computation.12 | async-start | bytes 1179648 | tf_op jit(solution)/shard_map/reduce_scatter | solution.py:120
  505.0 6.0 collective-permute-start.2
  508.4 8.0 %copy-start = (bf16[2048,256]{1,0:T(8,128)(2,1)S(1)}, bf16[2048,256]{1,0:T(8,128)(2,1)}, u32[]{:S(2)}) copy-start(bf16[2048,256]{1,0:T(8,128)(2,1)} %all-gather.12.cloned.1.call-done) | copy-start | bytes 3145732
  508.4 7.8 %collective-permute-start.3 = (f32[128,512]{1,0:T(8,128)S(1)}, f32[128,512]{1,0:T(8,128)S(1)}, u32[]{:S(2)}, u32[]{:S(2)}) collective-permute-start(f32[128,512]{1,0:T(8,128)S(1)} %bitcast.115), channel_id=1, source_target_pairs={{0,8},{8,16},{16,24},{24,32},{32,40},{40,48},{48,56},{56,64},{64,7... | collective-permute-start | bytes 786440 | tf_op jit(solution)/shard_map/ppermute | solution.py:14
  516.3 1.2 copy-start.4
Sparse Core Ops, SparseCore 0:
  10.0 49.8 all-gather.7
  63.3 83.5 all-gather.11
  150.2 80.3 all-gather.9
  232.4 43.2 all-gather.13
  279.0 83.5 all-gather.15
  364.4 43.2 all-gather.19
  411.1 83.5 all-gather.17
  500.3 45.0 reduce-scatter.3
  548.8 46.1 reduce-scatter.5
  598.3 45.2 reduce-scatter.7
where the time goes:
time: 651 us; the launch traced here: 650 us
  waiting for transfers between devices  604 us (93%)
  matrix products  15.5 us (2%)
  between operations  14.4 us (2%)
  starting transfers between devices  11.1 us (2%)
    all_gather x1, waiting for transfers between devices, per_device(): lax.all_gather(w_out, 'seq', axis=0, tiled=True)  86.9 us
    all_gather x1, waiting for transfers between devices, per_device(): lax.all_gather(w_value, 'seq', axis=0, tiled=True)  86.9 us
    all_gather x1, waiting for transfers between devices, per_device(): lax.all_gather(w_query, 'seq', axis=0, tiled=True)  86.8 us
    all_gather x1, waiting for transfers between devices, per_device(): lax.all_gather(w_key, 'seq', axis=0, tiled=True)  81.7 us
    reduce_scatter x1, waiting for transfers between devices, per_device(): lax.psum_scatter(times_transpose(d_query_flat, wq).astype(jnp.bfloat16),...  49.6 us
    reduce_scatter x1, waiting for transfers between devices, per_device(): lax.psum_scatter(source_term.astype(jnp.bfloat16), 'head', scatter_dimens...  48.6 us
    all_gather x1, waiting for transfers between devices, per_device(): piece = lax.all_gather(source, 'head', axis=1, tiled=True)  46.8 us
    all_gather x1, waiting for transfers between devices, per_device(): lax.all_gather(cotangent, 'head', axis=1, tiled=True)  43.1 us
  transfers between devices with their start and end apart: 14, of which 11 were waited for; matrix products, arithmetic and copies ran while one was open for 2% of the time, Pallas kernels for 0%

commit v1 on v0

--- a/solution.py
+++ b/solution.py
@@ -33,9 +33,18 @@
     blocks = rows // BLOCK
     right_rows = (MAXW - 1) * BLOCK
     scale = HEAD_DIM ** (-0.5)
+    object_apply = lambda local_x: jnp.concatenate(
+        lax.all_to_all(
+            jnp.stack(lax.psum(1, axis_name="seq") * [local_x], 0),
+            axis_name="seq",
+            split_axis=0,
+            concat_axis=0,
+        ),
+        0,
+    )
     wq, wk, wv, wo = (
         lax.all_gather(w_query, "seq", axis=0, tiled=True),
-        lax.all_gather(w_key, "seq", axis=0, tiled=True),
+        object_apply(w_key),
         lax.all_gather(w_value, "seq", axis=0, tiled=True),
         lax.all_gather(w_out, "seq", axis=0, tiled=True),
     )

time: 651 us -> 589 us (0.905)
  waiting for transfers between devices: 604 us -> 526 us
  starting transfers between devices: 11.1 us -> 27.7 us
    all_gather x1 -> x0, waiting for transfers between devices: 81.7 us -> none  [per_device(): lax.all_gather(w_key, 'seq', axis=0, tiled=True)]
    all_to_all x0 -> x1, starting transfers between devices: none -> 16.6 us  [per_device(): lax.all_to_all(jnp.stack(lax.psum(1, axis_name='seq') * [local_x], 0), ax...]
  transfers between devices with their start and end apart: 14 -> 14, of which waited for: 11 -> 10; matrix products, arithmetic and copies ran while one was open for 2% -> 3% of each run, Pallas kernels for 0% -> 0%
where the time goes in v1:
time: 589 us
  waiting for transfers between devices  526 us (89%)
  starting transfers between devices  27.7 us (5%)
  matrix products  16.4 us (3%)
  between operations  14.2 us (2%)
    all_gather x1, waiting for transfers between devices, per_device(): lax.all_gather(w_value, 'seq', axis=0, tiled=True)  87.2 us
    all_gather x1, waiting for transfers between devices, per_device(): lax.all_gather(w_out, 'seq', axis=0, tiled=True)  86.8 us
    all_gather x1, waiting for transfers between devices, per_device(): lax.all_gather(w_query, 'seq', axis=0, tiled=True)  86.8 us
    all_gather x1, waiting for transfers between devices, per_device(): piece = lax.all_gather(source, 'head', axis=1, tiled=True)  51.1 us
    reduce_scatter x1, waiting for transfers between devices, per_device(): lax.psum_scatter(times_transpose(d_query_flat, wq).astype(jnp.bfloat16),...  49.4 us
    reduce_scatter x1, waiting for transfers between devices, per_device(): lax.psum_scatter(source_term.astype(jnp.bfloat16), 'head', scatter_dimens...  48.8 us
    all_gather x1, waiting for transfers between devices, per_device(): lax.all_gather(cotangent, 'head', axis=1, tiled=True)  43.1 us
    all_gather x1, waiting for transfers between devices, per_device(): lax.all_gather(target, 'head', axis=1, tiled=True)  37 us
  transfers between devices with their start and end apart: 14, of which 10 were waited for; matrix products, arithmetic and copies ran while one was open for 3% of the time, Pallas kernels for 0%

profile of v1, /device:TPU:8, one launch (start us, length us, event | category | flops | bytes accessed | tf_op | source)
XLA Modules:
  0.0 588.9 jit_solution(7841244516481361144)
XLA Ops:
  10.6 1.8 stack.2
  12.4 16.6 %all-to-all-start = ((bf16[64,32,256]{2,1,0:T(8,128)(2,1)}), bf16[64,32,256]{2,1,0:T(8,128)(2,1)S(1)}, u32[]{:S(2)}, u32[]{:S(2)}) async-start(bf16[64,32,256]{2,1,0:T(8,128)(2,1)} %stack.2), calls=%async_computation | async-start | bytes 2097152 | tf_op jit(solution)/shard_map/all_to_all | solution.py:37
  30.1 51.1 %all-gather.7.cloned.1.call-done = bf16[256,2048]{1,0:T(8,128)(2,1)} async-done(((bf16[256,256]{1,0:T(8,128)(2,1)}), bf16[256,2048]{1,0:T(8,128)(2,1)}) %all-gather.7.cloned.1.call-update) | async-done | bytes 1048592 | tf_op jit(solution)/shard_map/all_gather | solution.py:52
  81.2 87.2 %all-gather.9.cloned.1.call-done = bf16[2048,256]{1,0:T(8,128)(2,1)} async-done(((bf16[32,256]{1,0:T(8,128)(2,1)}), bf16[2048,256]{1,0:T(8,128)(2,1)}) %all-gather.9.cloned.1.call-update) | async-done | bytes 1048592 | tf_op jit(solution)/shard_map/all_gather | solution.py:48
  168.5 2.1 convolution_convert_fusion.6
  171.2 2.1 collective-permute-start
  173.3 3.4 collective-permute-start.1
  176.8 37.0 %all-gather.11.cloned.1.call-done = bf16[256,2048]{1,0:T(8,128)(2,1)} async-done(((bf16[256,256]{1,0:T(8,128)(2,1)}), bf16[256,2048]{1,0:T(8,128)(2,1)}) %all-gather.11.cloned.1.call-update) | async-done | bytes 1048592 | tf_op jit(solution)/shard_map/all_gather | solution.py:51
  213.8 86.8 %all-gather.13.cloned.1.call-done = bf16[2048,256]{1,0:T(8,128)(2,1)} async-done(((bf16[32,256]{1,0:T(8,128)(2,1)}), bf16[2048,256]{1,0:T(8,128)(2,1)}) %all-gather.13.cloned.1.call-update) | async-done | bytes 1048592 | tf_op jit(solution)/shard_map/all_gather | solution.py:46
  300.6 2.1 convolution_convert_fusion.5
  302.6 43.1 %all-gather.17.cloned.1.call-done = bf16[256,2048]{1,0:T(8,128)(2,1)} async-done(((bf16[256,256]{1,0:T(8,128)(2,1)}), bf16[256,2048]{1,0:T(8,128)(2,1)}) %all-gather.17.cloned.1.call-update) | async-done | bytes 1048592 | tf_op jit(solution)/shard_map/all_gather | solution.py:94
  345.7 86.8 %all-gather.15.cloned.1.call-done = bf16[2048,256]{1,0:T(8,128)(2,1)} async-done(((bf16[32,256]{1,0:T(8,128)(2,1)}), bf16[2048,256]{1,0:T(8,128)(2,1)}) %all-gather.15.cloned.1.call-update) | async-done | bytes 1048592 | tf_op jit(solution)/shard_map/all_gather | solution.py:49
  432.5 2.1 convolution_convert_fusion.4
  434.9 1.4 fusion.27
  437.5 1.5 convolution_convert_fusion.1
  439.0 1.6 fusion.7
  440.9 1.5 convolution_convert_fusion
  444.4 3.1 collective-permute-start.2
  447.8 2.1 collective-permute-start.3
  450.4 5.2 collective-permute-done.3
  456.2 1.5 fusion.1
  457.7 26.5 %reduce-scatter.4.cloned.1.call-done = bf16[256,256]{1,0:T(8,128)(2,1)} async-done(((bf16[256,2048]{1,0:T(8,128)(2,1)}), bf16[256,256]{1,0:T(8,128)(2,1)}) %reduce-scatter.4.cloned.1.call-update) | async-done | bytes 131088 | tf_op jit(solution)/shard_map/reduce_scatter | solution.py:85
  484.2 49.4 %reduce-scatter.6.cloned.1.call-done = bf16[256,256]{1,0:T(8,128)(2,1)} async-done(((bf16[256,2048]{1,0:T(8,128)(2,1)}), bf16[256,256]{1,0:T(8,128)(2,1)}) %reduce-scatter.6.cloned.1.call-update) | async-done | bytes 131088 | tf_op jit(solution)/shard_map/reduce_scatter | solution.py:118
  533.6 48.8 %reduce-scatter.8.cloned.1.call-done = bf16[256,256]{1,0:T(8,128)(2,1)} async-done(((bf16[256,2048]{1,0:T(8,128)(2,1)}), bf16[256,256]{1,0:T(8,128)(2,1)}) %reduce-scatter.8.cloned.1.call-update) | async-done | bytes 131088 | tf_op jit(solution)/shard_map/reduce_scatter | solution.py:129
  (61 shorter events, 10.2 us)
Async XLA Ops:
  7.2 22.4 %copy-start.4 = (s32[4]{0:T(128)S(1)}, s32[4]{0:T(128)}, u32[]{:S(2)}) copy-start(s32[4]{0:T(128)} %param.20) | copy-start | bytes 52
  7.2 22.4 %copy-start.5 = (s32[4]{0:T(128)S(1)}, s32[4]{0:T(128)}, u32[]{:S(2)}) copy-start(s32[4]{0:T(128)} %param.19) | copy-start | bytes 52
  7.2 74.0 %all-gather.7.cloned.1.call-start = ((), (), s32[]{:S(2)}) async-start(), calls=%async_computation.4 | async-start | bytes 1179648 | tf_op jit(solution)/shard_map/all_gather | solution.py:52
  7.9 160.5 %all-gather.9.cloned.1.call-start = ((), (), s32[]{:S(2)}) async-start(), calls=%async_computation.5 | async-start | bytes 1064960 | tf_op jit(solution)/shard_map/all_gather | solution.py:48
  8.7 205.1 %all-gather.11.cloned.1.call-start = ((), (), s32[]{:S(2)}) async-start(), calls=%async_computation.6 | async-start | bytes 1179648 | tf_op jit(solution)/shard_map/all_gather | solution.py:51
  9.4 291.2 %all-gather.13.cloned.1.call-start = ((), (), s32[]{:S(2)}) async-start(), calls=%async_computation.7 | async-start | bytes 1064960 | tf_op jit(solution)/shard_map/all_gather | solution.py:46
  10.0 335.7 %all-gather.17.cloned.1.call-start = ((), (), s32[]{:S(2)}) async-start(), calls=%async_computation.10 | async-start | bytes 1179648 | tf_op jit(solution)/shard_map/all_gather | solution.py:94
  12.4 158.1 %all-to-all-start = ((bf16[64,32,256]{2,1,0:T(8,128)(2,1)}), bf16[64,32,256]{2,1,0:T(8,128)(2,1)S(1)}, u32[]{:S(2)}, u32[]{:S(2)}) async-start(bf16[64,32,256]{2,1,0:T(8,128)(2,1)} %stack.2), calls=%async_computation | async-start | bytes 2097152 | tf_op jit(solution)/shard_map/all_to_all | solution.py:37
  29.0 403.5 %all-gather.15.cloned.1.call-start = ((), (), s32[]{:S(2)}) async-start(), calls=%async_computation.8 | async-start | bytes 1064960 | tf_op jit(solution)/shard_map/all_gather | solution.py:49
  29.5 454.7 %reduce-scatter.4.cloned.1.call-start = ((), (), s32[]{:S(2)}) async-start(), calls=%async_computation.9 | async-start | bytes 1179648 | tf_op jit(solution)/shard_map/reduce_scatter | solution.py:85
  81.2 89.3 %copy-start.3 = (bf16[256,2048]{1,0:T(8,128)(2,1)S(1)}, bf16[256,2048]{1,0:T(8,128)(2,1)}, u32[]{:S(2)}) copy-start(bf16[256,2048]{1,0:T(8,128)(2,1)} %all-gather.7.cloned.1.call-done) | copy-start | bytes 3145732
  171.2 263.4 %collective-permute-start = (bf16[64,512]{0,1:T(8,128)(2,1)S(1)}, bf16[64,512]{0,1:T(8,128)(2,1)S(1)}, u32[]{:S(2)}, u32[]{:S(2)}) collective-permute-start(bf16[64,512]{0,1:T(8,128)(2,1)S(1)} %fusion.13), channel_id=1, source_target_pairs={{0,8},{8,16},{16,24},{24,32},{32,40},{40,48},{48,56},{56,64},{64,7... | collective-permute-start | bytes 196616 | tf_op jit(solution)/shard_map/ppermute | solution.py:14
  173.3 261.2 %collective-permute-start.1 = (bf16[128,512]{0,1:T(8,128)(2,1)S(1)}, bf16[128,512]{0,1:T(8,128)(2,1)S(1)}, u32[]{:S(2)}, u32[]{:S(2)}) collective-permute-start(bf16[128,512]{0,1:T(8,128)(2,1)S(1)} %pad_maximum_fusion.2), channel_id=1, source_target_pairs={{8,0},{16,8},{24,16},{32,24},{40,32},{48,40},{56,48},{64,56},{72,6... | collective-permute-start | bytes 393224 | tf_op jit(solution)/shard_map/ppermute | solution.py:14
  436.3 1.2 copy-start.2
  439.0 94.6 %reduce-scatter.6.cloned.1.call-start = ((), (), s32[]{:S(2)}) async-start(), calls=%async_computation.11 | async-start | bytes 1179648 | tf_op jit(solution)/shard_map/reduce_scatter | solution.py:118
  439.0 1.8 copy-start.1
  442.4 140.0 %reduce-scatter.8.cloned.1.call-start = ((), (), s32[]{:S(2)}) async-start(), calls=%async_computation.12 | async-start | bytes 1179648 | tf_op jit(solution)/shard_map/reduce_scatter | solution.py:129
  444.4 6.0 %collective-permute-start.2 = (f32[64,512]{1,0:T(8,128)S(1)}, f32[64,512]{1,0:T(8,128)S(1)}, u32[]{:S(2)}, u32[]{:S(2)}) collective-permute-start(f32[64,512]{1,0:T(8,128)S(1)} %bitcast.123), channel_id=1, source_target_pairs={{8,0},{16,8},{24,16},{32,24},{40,32},{48,40},{56,48},{64,56},{72,6... | collective-permute-start | bytes 393224 | tf_op jit(solution)/shard_map/ppermute | solution.py:14
  447.8 8.0 %copy-start = (bf16[2048,256]{1,0:T(8,128)(2,1)S(1)}, bf16[2048,256]{1,0:T(8,128)(2,1)}, u32[]{:S(2)}) copy-start(bf16[2048,256]{1,0:T(8,128)(2,1)} %all-gather.9.cloned.1.call-done) | copy-start | bytes 3145732
  447.8 7.8 %collective-permute-start.3 = (f32[128,512]{1,0:T(8,128)S(1)}, f32[128,512]{1,0:T(8,128)S(1)}, u32[]{:S(2)}, u32[]{:S(2)}) collective-permute-start(f32[128,512]{1,0:T(8,128)S(1)} %bitcast.118), channel_id=1, source_target_pairs={{0,8},{8,16},{16,24},{24,32},{32,40},{40,48},{48,56},{56,64},{64,7... | collective-permute-start | bytes 786440 | tf_op jit(solution)/shard_map/ppermute | solution.py:14
Sparse Core Ops, SparseCore 0:
  10.0 71.1 all-gather.6
  84.6 83.8 all-gather.8
  170.5 43.2 all-gather.10
  217.0 83.5 all-gather.12
  302.4 43.2 all-gather.16
  348.9 83.5 all-gather.14
  439.1 45.0 reduce-scatter.3
  487.6 45.9 reduce-scatter.5
  537.0 45.3 reduce-scatter.7
